TPU v7x, 256 devices: a whole 4x4x8 slice. The times are simulated.
256 devices in a mesh: section: 4 (over y_lo, core), dp: 8 (over z), mp: 8 (over y_hi, x).
Axes of the slice: x: 4, y: 4 (y_hi: 2, y_lo: 2; y = y_hi * 2 + y_lo), z: 8, core: 2. Of those that a mesh axis runs over, the one named last changes fastest.
Arguments:
- encoder_rows: bfloat16 [96, 256, 4096], P(('section', 'dp')), may hold values from -6 to 6
- w_key: bfloat16 [4096, 4096], P(('section', 'dp'), 'mp'), may hold values from -0.09375 to 0.09375
- w_value: bfloat16 [4096, 4096], P(('section', 'dp'), 'mp'), may hold values from -0.09375 to 0.09375
- query: bfloat16 [128, 128, 4096], P(('section', 'dp'), None, 'mp'), may hold values from -80 to 80
- grad_context: bfloat16 [128, 128, 4096], P(('section', 'dp'), None, 'mp'), may hold values from -6 to 6
- source: int32 [128], replicated, may hold values from 0 to 95, as said below
Outputs:
- context: bfloat16 [128, 128, 4096], P(('section', 'dp'), None, 'mp')
- grad_query: bfloat16 [128, 128, 4096], P(('section', 'dp'), None, 'mp')
- grad_kv_weights: float32 [2, 4096, 4096], P(None, ('section', 'dp'), 'mp')
Inputs may be any that keep to these rules, and one draw needn't show every extreme that they name: `source`: the sequences of one section index (the 32 consecutive sequences held at that section index) read only examples held at the same section index; the 4 sequences of one device read examples held at 4 different dp indices.
All inputs are finite; a program needn't handle non-finite values.
Results may differ from a plain program's by a relative error of at most 0.025.
The roundings to bfloat16 on the way count: a program that leaves them out, or rounds other values in their place, can miss the bound.
Values may be sent and summed in bfloat16 or wider, within the bound.
A program may use at most 128 MiB of HBM per device.

v0:
```python
import jax
import jax.numpy as jnp
from jax import lax
from jax.sharding import PartitionSpec as P

HEAD_DIM = 64


def per_device(encoder_rows, w_key, w_value, query, grad_context, source):
    ex_dev, seq_len, width = encoder_rows.shape
    dec_dev, q_rows, inner_dev = query.shape
    heads_dev = inner_dev // HEAD_DIM
    n_dp = lax.axis_size("dp")
    section_idx = lax.axis_index("section")
    dp_idx = lax.axis_index("dp")
    flat = encoder_rows.reshape(ex_dev * seq_len, width)
    key_acc = jnp.dot(
        flat,
        lax.all_gather(w_key, ("section", "dp"), axis=0, tiled=True),
        preferred_element_type=jnp.float32,
    )
    value_acc = jnp.dot(
        flat,
        lax.all_gather(w_value, ("section", "dp"), axis=0, tiled=True),
        preferred_element_type=jnp.float32,
    )
    keys = key_acc.astype(jnp.bfloat16).reshape(ex_dev, seq_len, inner_dev)
    values = value_acc.astype(jnp.bfloat16).reshape(ex_dev, seq_len, inner_dev)
    per_section = n_dp * dec_dev
    row_plan = lax.dynamic_slice_in_dim(source, section_idx * per_section, per_section).reshape(
        n_dp, dec_dev
    )
    holder_dp = row_plan // ex_dev - section_idx * n_dp
    local_ex = row_plan % ex_dev
    mine = holder_dp == dp_idx
    wanted = mine[:, :, None] & (
        local_ex[:, :, None] == jnp.arange(ex_dev, dtype=jnp.int32)[None, None, :]
    )
    pick = jnp.sum(wanted.astype(jnp.float32), axis=1).astype(jnp.bfloat16)
    my_holder = lax.dynamic_index_in_dim(holder_dp, dp_idx, 0, keepdims=False)
    send_keys = jnp.einsum("pk,ksc->psc", pick, keys, preferred_element_type=jnp.float32).astype(
        jnp.bfloat16
    )
    send_values = jnp.einsum(
        "pk,ksc->psc", pick, values, preferred_element_type=jnp.float32
    ).astype(jnp.bfloat16)
    recv_keys, recv_values = (
        lax.all_to_all(send_keys, "dp", split_axis=0, concat_axis=0, tiled=True),
        lax.all_to_all(send_values, "dp", split_axis=0, concat_axis=0, tiled=True),
    )
    tile_keys = jnp.take(recv_keys, my_holder, axis=0)
    tile_values = jnp.take(recv_values, my_holder, axis=0)
    q_four = query.reshape(dec_dev, q_rows, heads_dev, HEAD_DIM)
    g_four = grad_context.reshape(dec_dev, q_rows, heads_dev, HEAD_DIM)
    k_four = tile_keys.reshape(dec_dev, seq_len, heads_dev, HEAD_DIM)
    v_four = tile_values.reshape(dec_dev, seq_len, heads_dev, HEAD_DIM)
    scores = jnp.einsum("nthc,nuhc->nhtu", q_four, k_four, preferred_element_type=jnp.float32)
    top = jnp.max(scores, axis=-1, keepdims=True)
    expo = jnp.exp(scores - top)
    weights = expo / jnp.sum(expo, axis=-1, keepdims=True)
    probs = weights.astype(jnp.bfloat16)
    context = jnp.einsum(
        "nhtu,nuhc->nthc", probs, v_four, preferred_element_type=jnp.float32
    ).astype(jnp.bfloat16)
    dprobs = jnp.einsum("nthc,nuhc->nhtu", g_four, v_four, preferred_element_type=jnp.float32)
    delta = jnp.sum(weights * dprobs, axis=-1, keepdims=True)
    score_grads = (weights * (dprobs - delta)).astype(jnp.bfloat16)
    grad_query = jnp.einsum(
        "nhtu,nuhc->nthc", score_grads, k_four, preferred_element_type=jnp.float32
    ).astype(jnp.bfloat16)
    key_terms = jnp.einsum(
        "nhtu,nthc->nuhc", score_grads, q_four, preferred_element_type=jnp.float32
    ).astype(jnp.bfloat16)
    value_terms = jnp.einsum(
        "nhtu,nthc->nuhc", probs, g_four, preferred_element_type=jnp.float32
    ).astype(jnp.bfloat16)
    key_terms = key_terms.reshape(dec_dev, seq_len, inner_dev)
    value_terms = value_terms.reshape(dec_dev, seq_len, inner_dev)
    to_holder = (my_holder[:, None] == jnp.arange(n_dp, dtype=jnp.int32)[None, :]).astype(
        jnp.bfloat16
    )
    back_keys = jnp.einsum(
        "np,nsc->psc", to_holder, key_terms, preferred_element_type=jnp.float32
    ).astype(jnp.bfloat16)
    back_values = jnp.einsum(
        "np,nsc->psc", to_holder, value_terms, preferred_element_type=jnp.float32
    ).astype(jnp.bfloat16)
    ret_keys, ret_values = (
        lax.all_to_all(back_keys, "dp", split_axis=0, concat_axis=0, tiled=True),
        lax.all_to_all(back_values, "dp", split_axis=0, concat_axis=0, tiled=True),
    )
    summed_keys = jnp.einsum("pk,psc->ksc", pick, ret_keys, preferred_element_type=jnp.float32)
    summed_values = jnp.einsum("pk,psc->ksc", pick, ret_values, preferred_element_type=jnp.float32)
    grad_keys = summed_keys.astype(jnp.bfloat16).reshape(ex_dev * seq_len, inner_dev)
    grad_values = summed_values.astype(jnp.bfloat16).reshape(ex_dev * seq_len, inner_dev)
    part_keys = lax.dot_general(
        flat, grad_keys, (((0,), (0,)), ((), ())), preferred_element_type=jnp.float32
    )
    part_values = lax.dot_general(
        flat, grad_values, (((0,), (0,)), ((), ())), preferred_element_type=jnp.float32
    )
    grad_rows = lax.psum_scatter(
        jnp.concatenate([part_keys, part_values], axis=1).astype(jnp.bfloat16),
        ("section", "dp"),
        scatter_dimension=0,
        tiled=True,
    ).astype(jnp.float32)
    grad_kv_weights = jnp.stack([grad_rows[:, :inner_dev], grad_rows[:, inner_dev:]], axis=0)
    return (
        context.reshape(dec_dev, q_rows, inner_dev),
        grad_query.reshape(dec_dev, q_rows, inner_dev),
        grad_kv_weights,
    )


def solution(mesh):
    return jax.shard_map(
        per_device,
        mesh=mesh,
        in_specs=(
            P(("section", "dp"), None, None),
            P(("section", "dp"), "mp"),
            P(("section", "dp"), "mp"),
            P(("section", "dp"), None, "mp"),
            P(("section", "dp"), None, "mp"),
            P(),
        ),
        out_specs=(
            P(("section", "dp"), None, "mp"),
            P(("section", "dp"), None, "mp"),
            P(None, ("section", "dp"), "mp"),
        ),
        check_vma=False,
    )
```

profile of v0, /device:TPU:1, one launch (start us, length us, event | category | flops | bytes accessed | tf_op | source)
XLA Modules:
  0.0 623.1 jit_solution(6543163994647986004)
XLA Ops:
  10.6 102.7 %all-gather.3.cloned.1.call-done = bf16[4096,512]{1,0:T(8,128)(2,1)} async-done(((bf16[128,512]{1,0:T(8,128)(2,1)}), bf16[4096,512]{1,0:T(8,128)(2,1)}) %all-gather.3.cloned.1.call-update) | async-done | bytes 4194320 | tf_op jit(solution)/shard_map/all_gather | solution.py:24
  113.3 7.4 %convolution_convert_fusion.7 = bf16[768,512]{1,0:T(8,128)(2,1)S(1)} fusion(bf16[768,4096]{1,0:T(8,128)(2,1)} %bitcast.106, bf16[4096,512]{1,0:T(8,128)(2,1)} %all-gather.3.cloned.1.call-done), kind=kOutput, calls=%fused_computation.31 | convolution fusion | flops 3221618688 | bytes 11272192 | tf_op jit(solution)/shard_map/dot_general | solution.py:22
  121.8 2.0 copy.86
  123.9 10.4 %all-to-all-start = ((bf16[8,256,512]{2,1,0:T(8,128)(2,1)}), bf16[8,256,512]{2,1,0:T(8,128)(2,1)S(1)}, u32[]{:S(2)}, u32[]{:S(2)}) async-start(bf16[8,256,512]{2,1,0:T(8,128)(2,1)} %copy.86), calls=%async_computation | async-start | bytes 4194304 | tf_op jit(solution)/shard_map/all_to_all | solution.py:49
  134.2 108.1 %all-gather.5.cloned.1.call-done = bf16[4096,512]{1,0:T(8,128)(2,1)} async-done(((bf16[128,512]{1,0:T(8,128)(2,1)}), bf16[4096,512]{1,0:T(8,128)(2,1)}) %all-gather.5.cloned.1.call-update) | async-done | bytes 4194320 | tf_op jit(solution)/shard_map/all_gather | solution.py:19
  242.3 7.4 %convolution_convert_fusion.6 = bf16[768,512]{1,0:T(8,128)(2,1)S(1)} fusion(bf16[768,4096]{1,0:T(8,128)(2,1)} %bitcast.107, bf16[4096,512]{1,0:T(8,128)(2,1)} %all-gather.5.cloned.1.call-done), kind=kOutput, calls=%fused_computation.30 | convolution fusion | flops 3221618688 | bytes 11272192 | tf_op jit(solution)/shard_map/dot_general | solution.py:17
  252.8 10.6 %all-to-all-start.1 = ((bf16[8,256,512]{2,1,0:T(8,128)(2,1)}), bf16[8,256,512]{2,1,0:T(8,128)(2,1)}, u32[]{:S(2)}, u32[]{:S(2)}) async-start(bf16[8,256,512]{2,1,0:T(8,128)(2,1)} %copy.89), calls=%async_computation.1 | async-start | bytes 4194304 | tf_op jit(solution)/shard_map/all_to_all | solution.py:48
  266.8 48.4 %all-to-all-done.1 = bf16[8,256,512]{2,1,0:T(8,128)(2,1)} async-done(((bf16[8,256,512]{2,1,0:T(8,128)(2,1)}), bf16[8,256,512]{2,1,0:T(8,128)(2,1)}, u32[]{:S(2)}, u32[]{:S(2)}) %all-to-all-start.1) | async-done | bytes 2097184 | tf_op jit(solution)/shard_map/all_to_all | solution.py:48
  315.3 2.2 gather_fusion.1
  317.5 2.4 broadcast_select_fusion
  322.7 3.4 fusion.40
  326.1 3.3 fusion.3
  332.5 2.7 copy.96
  335.1 2.1 convolution_convert_fusion.1
  339.3 4.3 all-to-all-start.2
  343.6 4.1 convolution_convert_fusion.4
  347.8 2.6 copy.101
  350.4 2.1 convolution_convert_fusion
  352.6 2.0 copy.102
  354.6 37.2 %all-to-all-done.2 = bf16[8,256,512]{2,1,0:T(8,128)(2,1)} async-done(((bf16[8,256,512]{2,1,0:T(8,128)(2,1)}), bf16[8,256,512]{2,1,0:T(8,128)(2,1)}, u32[]{:S(2)}, u32[]{:S(2)}) %all-to-all-start.2) | async-done | bytes 2097184 | tf_op jit(solution)/shard_map/all_to_all | solution.py:89
  391.8 4.9 all-to-all-start.3
  397.0 3.0 fusion.14
  400.0 8.1 %fusion.1 = bf16[4096,512]{0,1:T(8,128)(2,1)} fusion(bf16[3,256,4096]{2,1,0:T(8,128)(2,1)} %param.8, bf16[3,256,512]{2,0,1:T(4,128)(2,1)S(1)} %fusion.14), kind=kOutput, calls=%fused_computation.6 | convolution fusion | flops 3223322624 | bytes 11272192 | tf_op jit(solution)/shard_map/dot_general | solution.py:96
  408.1 38.4 %all-to-all-done.3 = bf16[8,256,512]{2,1,0:T(8,128)(2,1)} async-done(((bf16[8,256,512]{2,1,0:T(8,128)(2,1)}), bf16[8,256,512]{2,1,0:T(8,128)(2,1)}, u32[]{:S(2)}, u32[]{:S(2)}) %all-to-all-start.3) | async-done | bytes 2097184 | tf_op jit(solution)/shard_map/all_to_all | solution.py:90
  446.4 3.0 fusion.17
  449.5 8.1 %fusion.2 = bf16[4096,512]{0,1:T(8,128)(2,1)} fusion(bf16[3,256,4096]{2,1,0:T(8,128)(2,1)} %param.8, bf16[3,256,512]{2,0,1:T(4,128)(2,1)S(1)} %fusion.17), kind=kOutput, calls=%fused_computation.7 | convolution fusion | flops 3223322624 | bytes 11272192 | tf_op jit(solution)/shard_map/dot_general | solution.py:99
  457.5 7.8 %pad_maximum_fusion = bf16[4096,1024]{0,1:T(8,128)(2,1)} fusion(bf16[4096,512]{0,1:T(8,128)(2,1)} %fusion.2, bf16[4096,512]{0,1:T(8,128)(2,1)} %fusion.1), kind=kLoop, calls=%fused_computation.3 | loop fusion | flops 16777216 | bytes 16777216 | tf_op jit(solution)/shard_map/concatenate | solution.py:103
  465.4 12.0 %copy.112 = bf16[4096,1024]{1,0:T(8,128)(2,1)} copy(bf16[4096,1024]{0,1:T(8,128)(2,1)} %pad_maximum_fusion) | data formatting | bytes 16777216
  477.4 3.8 convolution_convert_fusion.9
  481.2 2.0 copy.105
  484.5 2.0 copy.106
  486.5 127.8 %reduce-scatter.4.cloned.1.call-done = bf16[128,1024]{1,0:T(8,128)(2,1)} async-done(((bf16[4096,1024]{1,0:T(8,128)(2,1)}), bf16[128,1024]{1,0:T(8,128)(2,1)}) %reduce-scatter.4.cloned.1.call-update) | async-done | bytes 262160
  (49 shorter events, 22.6 us)
Async XLA Ops:
  7.2 106.2 %all-gather.3.cloned.1.call-start = ((), (), s32[]{:S(2)}) async-start(), calls=%async_computation.5 | async-start | bytes 4325376 | tf_op jit(solution)/shard_map/all_gather | solution.py:24
  7.9 234.4 %all-gather.5.cloned.1.call-start = ((), (), s32[]{:S(2)}) async-start(), calls=%async_computation.6 | async-start | bytes 4325376 | tf_op jit(solution)/shard_map/all_gather | solution.py:19
  123.9 128.9 %all-to-all-start = ((bf16[8,256,512]{2,1,0:T(8,128)(2,1)}), bf16[8,256,512]{2,1,0:T(8,128)(2,1)S(1)}, u32[]{:S(2)}, u32[]{:S(2)}) async-start(bf16[8,256,512]{2,1,0:T(8,128)(2,1)} %copy.86), calls=%async_computation | async-start | bytes 4194304 | tf_op jit(solution)/shard_map/all_to_all | solution.py:49
  250.8 12.6 %copy-start.4 = (bf16[4,128,512]{2,1,0:T(8,128)(2,1)S(1)}, bf16[4,128,512]{2,1,0:T(8,128)(2,1)}, u32[]{:S(2)}) copy-start(bf16[4,128,512]{2,1,0:T(8,128)(2,1)} %param.11) | copy-start | bytes 1572868
  252.8 62.5 %all-to-all-start.1 = ((bf16[8,256,512]{2,1,0:T(8,128)(2,1)}), bf16[8,256,512]{2,1,0:T(8,128)(2,1)}, u32[]{:S(2)}, u32[]{:S(2)}) async-start(bf16[8,256,512]{2,1,0:T(8,128)(2,1)} %copy.89), calls=%async_computation.1 | async-start | bytes 4194304 | tf_op jit(solution)/shard_map/all_to_all | solution.py:48
  263.7 59.1 %copy-start.1 = (bf16[4,128,512]{1,2,0:T(8,128)(2,1)}, bf16[4,128,512]{1,2,0:T(8,128)(2,1)S(1)}, u32[]{:S(2)}) copy-start(bf16[4,128,512]{1,2,0:T(8,128)(2,1)S(1)} %copy.91) | copy-start | bytes 1572868
  265.2 60.9 %copy-start.5 = (bf16[4,128,512]{1,2,0:T(8,128)(2,1)}, bf16[4,128,512]{1,2,0:T(8,128)(2,1)S(1)}, u32[]{:S(2)}) copy-start(bf16[4,128,512]{1,2,0:T(8,128)(2,1)S(1)} %copy.93) | copy-start | bytes 1572868
  322.7 3.4 copy-start.3
  326.1 3.5 copy-start
  329.5 1.1 copy-start.2
  339.3 52.5 %all-to-all-start.2 = ((bf16[8,256,512]{2,1,0:T(8,128)(2,1)}), bf16[8,256,512]{2,1,0:T(8,128)(2,1)}, u32[]{:S(2)}, u32[]{:S(2)}) async-start(bf16[8,256,512]{2,1,0:T(8,128)(2,1)} %copy.97), calls=%async_computation.2 | async-start | bytes 4194304 | tf_op jit(solution)/shard_map/all_to_all | solution.py:89
  391.8 54.6 %all-to-all-start.3 = ((bf16[8,256,512]{2,1,0:T(8,128)(2,1)}), bf16[8,256,512]{2,1,0:T(8,128)(2,1)}, u32[]{:S(2)}, u32[]{:S(2)}) async-start(bf16[8,256,512]{2,1,0:T(8,128)(2,1)} %copy.102), calls=%async_computation.3 | async-start | bytes 4194304 | tf_op jit(solution)/shard_map/all_to_all | solution.py:90
  396.7 217.6 %reduce-scatter.4.cloned.1.call-start = ((), (), s32[]{:S(2)}) async-start(), calls=%async_computation.7 | async-start | bytes 8650752
Sparse Core Ops, SparseCore 0:
  9.8 103.5 all-gather.2
  115.1 127.0 all-gather.4
  477.5 136.7 reduce-scatter.3
where the time goes:
time: 624 us; the launch traced here: 623 us
  waiting for transfers between devices  464 us (74%)
  matrix products  61.1 us (10%)
  local copies, waits for them, and re-layouts  40.5 us (6%)
  starting transfers between devices  30.5 us (5%)
  between operations  14 us (2%)
  other arithmetic  13 us (2%)
    unnamed x4, waiting for transfers between devices  129 us
    all_gather x1, waiting for transfers between devices, per_device(): lax.all_gather(w_key, ('section', 'dp'), axis=0, tiled=True)  108 us
    all_gather x1, waiting for transfers between devices, per_device(): lax.all_gather(w_value, ('section', 'dp'), axis=0, tiled=True)  103 us
    all_to_all x1, waiting for transfers between devices, per_device(): lax.all_to_all(send_keys, 'dp', split_axis=0, concat_axis=0, tiled=True)  48.4 us
    all_to_all x1, waiting for transfers between devices, per_device(): lax.all_to_all(back_values, 'dp', split_axis=0, concat_axis=0, tiled=True)  38.4 us
    all_to_all x1, waiting for transfers between devices, per_device(): lax.all_to_all(back_keys, 'dp', split_axis=0, concat_axis=0, tiled=True)  37.2 us
    unnamed x19, local copies, waits for them, and re-layouts  20.1 us
  transfers between devices with their start and end apart: 7, of which 6 were waited for; matrix products, arithmetic and copies ran while one was open for 9% of the time, Pallas kernels for 0%

commit v1 on v0

--- a/solution.py
+++ b/solution.py
@@ -21,7 +21,12 @@
     )
     value_acc = jnp.dot(
         flat,
-        lax.all_gather(w_value, ("section", "dp"), axis=0, tiled=True),
+        jnp.concatenate(
+            lax.all_to_all(
+                jnp.stack([w_value] * lax.axis_size(("section", "dp"))), ("section", "dp"), 0, 0
+            ),
+            axis=0,
+        ),
         preferred_element_type=jnp.float32,
     )
     keys = key_acc.astype(jnp.bfloat16).reshape(ex_dev, seq_len, inner_dev)

time: 624 us -> 604 us (0.968)
  waiting for transfers between devices: 464 us -> 436 us
    all_gather x1 -> x0, waiting for transfers between devices: 103 us -> none  [per_device(): lax.all_gather(w_value, ('section', 'dp'), axis=0, tiled=True)]
    all_to_all x1, waiting for transfers between devices: 0.01 us -> 44.6 us  [per_device(): lax.all_to_all(send_values, 'dp', split_axis=0, concat_axis=0, tiled=True)]
    all_gather x1, waiting for transfers between devices: 108 us -> 145 us  [per_device(): lax.all_gather(w_key, ('section', 'dp'), axis=0, tiled=True)]
    all_to_all x0 -> x1, starting transfers between devices: none -> 11.3 us  [per_device(): lax.all_to_all(jnp.stack([w_value] * lax.axis_size(('section', 'dp'))), (...]
    all_to_all x1, waiting for transfers between devices: 48.4 us -> 41.1 us  [per_device(): lax.all_to_all(send_keys, 'dp', split_axis=0, concat_axis=0, tiled=True)]
    unnamed x4 -> x3, waiting for transfers between devices: 129 us -> 128 us
    unnamed x19 -> x21, local copies, waits for them, and re-layouts: 20.1 us -> 20.1 us
  transfers between devices with their start and end apart: 7 -> 7, of which waited for: 6 -> 6; matrix products, arithmetic and copies ran while one was open for 9% -> 10% of each run, Pallas kernels for 0% -> 0%
where the time goes in v1:
time: 604 us; the launch traced here: 603 us
  waiting for transfers between devices  436 us (72%)
  matrix products  61.1 us (10%)
  local copies, waits for them, and re-layouts  43.9 us (7%)
  starting transfers between devices  35.7 us (6%)
  between operations  14.3 us (2%)
  other arithmetic  11.7 us (2%)
    all_gather x1, waiting for transfers between devices, per_device(): lax.all_gather(w_key, ('section', 'dp'), axis=0, tiled=True)  145 us
    unnamed x3, waiting for transfers between devices  128 us
    all_to_all x1, waiting for transfers between devices, per_device(): lax.all_to_all(send_values, 'dp', split_axis=0, concat_axis=0, tiled=True)  44.6 us
    all_to_all x1, waiting for transfers between devices, per_device(): lax.all_to_all(send_keys, 'dp', split_axis=0, concat_axis=0, tiled=True)  41.1 us
    all_to_all x1, waiting for transfers between devices, per_device(): lax.all_to_all(back_keys, 'dp', split_axis=0, concat_axis=0, tiled=True)  40.9 us
    all_to_all x1, waiting for transfers between devices, per_device(): lax.all_to_all(back_values, 'dp', split_axis=0, concat_axis=0, tiled=True)  36.8 us
    unnamed x21, local copies, waits for them, and re-layouts  20.1 us
  transfers between devices with their start and end apart: 7, of which 6 were waited for; matrix products, arithmetic and copies ran while one was open for 10% of the time, Pallas kernels for 0%

profile of v1, /device:TPU:1, one launch (start us, length us, event | category | flops | bytes accessed | tf_op | source)
XLA Modules:
  0.0 602.8 jit_solution(6927890814870697730)
XLA Ops:
  7.9 3.3 stack.8
  11.2 11.3 %all-to-all-start = ((bf16[32,128,512]{2,1,0:T(8,128)(2,1)}), bf16[32,128,512]{2,1,0:T(8,128)(2,1)}, u32[]{:S(2)}, u32[]{:S(2)}) async-start(bf16[32,128,512]{2,1,0:T(8,128)(2,1)} %stack.8), calls=%async_computation | async-start | bytes 8388608 | tf_op jit(solution)/shard_map/all_to_all | solution.py:25
  23.2 144.6 %all-gather.2.cloned.1.call-done = bf16[4096,512]{1,0:T(8,128)(2,1)} async-done(((bf16[128,512]{1,0:T(8,128)(2,1)}), bf16[4096,512]{1,0:T(8,128)(2,1)}) %all-gather.2.cloned.1.call-update) | async-done | bytes 4194320 | tf_op jit(solution)/shard_map/all_gather | solution.py:19
  167.9 7.4 %convolution_convert_fusion.6 = bf16[768,512]{1,0:T(8,128)(2,1)S(1)} fusion(bf16[768,4096]{1,0:T(8,128)(2,1)} %bitcast.107, bf16[4096,512]{1,0:T(8,128)(2,1)} %all-gather.2.cloned.1.call-done), kind=kOutput, calls=%fused_computation.30 | convolution fusion | flops 3221618688 | bytes 11272192 | tf_op jit(solution)/shard_map/dot_general | solution.py:17
  176.4 2.1 copy.89
  178.4 10.2 %all-to-all-start.2 = ((bf16[8,256,512]{2,1,0:T(8,128)(2,1)}), bf16[8,256,512]{2,1,0:T(8,128)(2,1)S(1)}, u32[]{:S(2)}, u32[]{:S(2)}) async-start(bf16[8,256,512]{2,1,0:T(8,128)(2,1)} %copy.89), calls=%async_computation.2 | async-start | bytes 4194304 | tf_op jit(solution)/shard_map/all_to_all | solution.py:53
  188.6 7.4 %convolution_convert_fusion.7 = bf16[768,512]{1,0:T(8,128)(2,1)S(1)} fusion(bf16[768,4096]{1,0:T(8,128)(2,1)} %bitcast.108, bf16[4096,512]{1,0:T(8,128)(2,1)} %bitcast.3), kind=kOutput, calls=%fused_computation.31 | convolution fusion | flops 3221618688 | bytes 11272192 | tf_op jit(solution)/shard_map/dot_general | solution.py:22
  199.1 41.1 %all-to-all-done.2 = bf16[8,256,512]{2,1,0:T(8,128)(2,1)S(1)} async-done(((bf16[8,256,512]{2,1,0:T(8,128)(2,1)}), bf16[8,256,512]{2,1,0:T(8,128)(2,1)S(1)}, u32[]{:S(2)}, u32[]{:S(2)}) %all-to-all-start.2) | async-done | bytes 2097184 | tf_op jit(solution)/shard_map/all_to_all | solution.py:53
  240.3 4.5 all-to-all-start.1
  248.2 44.6 %all-to-all-done.1 = bf16[8,256,512]{2,1,0:T(8,128)(2,1)} async-done(((bf16[8,256,512]{2,1,0:T(8,128)(2,1)}), bf16[8,256,512]{2,1,0:T(8,128)(2,1)}, u32[]{:S(2)}, u32[]{:S(2)}) %all-to-all-start.1) | async-done | bytes 2097184 | tf_op jit(solution)/shard_map/all_to_all | solution.py:54
  292.8 2.2 gather_fusion
  295.0 2.4 broadcast_select_fusion
  300.3 3.4 fusion.40
  303.6 3.3 fusion.3
  310.1 2.7 copy.96
  312.7 2.1 convolution_convert_fusion.1
  316.9 5.1 all-to-all-start.3
  321.9 4.1 convolution_convert_fusion.4
  326.0 2.6 copy.101
  328.7 2.1 convolution_convert_fusion
  332.9 40.9 %all-to-all-done.3 = bf16[8,256,512]{2,1,0:T(8,128)(2,1)} async-done(((bf16[8,256,512]{2,1,0:T(8,128)(2,1)}), bf16[8,256,512]{2,1,0:T(8,128)(2,1)}, u32[]{:S(2)}, u32[]{:S(2)}) %all-to-all-start.3) | async-done | bytes 2097184 | tf_op jit(solution)/shard_map/all_to_all | solution.py:94
  373.7 4.3 all-to-all-start.4
  378.3 3.0 fusion.14
  381.4 8.1 %fusion.1 = bf16[4096,512]{0,1:T(8,128)(2,1)} fusion(bf16[3,256,4096]{2,1,0:T(8,128)(2,1)} %param.8, bf16[3,256,512]{2,0,1:T(4,128)(2,1)S(1)} %fusion.14), kind=kOutput, calls=%fused_computation.6 | convolution fusion | flops 3223322624 | bytes 11272192 | tf_op jit(solution)/shard_map/dot_general | solution.py:101
  389.4 36.8 %all-to-all-done.4 = bf16[8,256,512]{2,1,0:T(8,128)(2,1)} async-done(((bf16[8,256,512]{2,1,0:T(8,128)(2,1)}), bf16[8,256,512]{2,1,0:T(8,128)(2,1)}, u32[]{:S(2)}, u32[]{:S(2)}) %all-to-all-start.4) | async-done | bytes 2097184 | tf_op jit(solution)/shard_map/all_to_all | solution.py:95
  426.2 3.0 fusion.17
  429.2 8.1 %fusion.2 = bf16[4096,512]{0,1:T(8,128)(2,1)} fusion(bf16[3,256,4096]{2,1,0:T(8,128)(2,1)} %param.8, bf16[3,256,512]{2,0,1:T(4,128)(2,1)S(1)} %fusion.17), kind=kOutput, calls=%fused_computation.7 | convolution fusion | flops 3223322624 | bytes 11272192 | tf_op jit(solution)/shard_map/dot_general | solution.py:104
  437.3 7.8 %pad_maximum_fusion = bf16[4096,1024]{0,1:T(8,128)(2,1)} fusion(bf16[4096,512]{0,1:T(8,128)(2,1)} %fusion.2, bf16[4096,512]{0,1:T(8,128)(2,1)} %fusion.1), kind=kLoop, calls=%fused_computation.3 | loop fusion | flops 16777216 | bytes 16777216 | tf_op jit(solution)/shard_map/concatenate | solution.py:108
  445.1 12.0 %copy.112 = bf16[4096,1024]{1,0:T(8,128)(2,1)} copy(bf16[4096,1024]{0,1:T(8,128)(2,1)} %pad_maximum_fusion) | data formatting | bytes 16777216
  457.2 3.8 convolution_convert_fusion.9
  460.9 2.0 copy.105
  466.3 127.4 %reduce-scatter.4.cloned.1.call-done = bf16[128,1024]{1,0:T(8,128)(2,1)} async-done(((bf16[4096,1024]{1,0:T(8,128)(2,1)}), bf16[128,1024]{1,0:T(8,128)(2,1)}) %reduce-scatter.4.cloned.1.call-update) | async-done | bytes 262160
  (51 shorter events, 24.6 us)
Async XLA Ops:
  7.2 160.7 %all-gather.2.cloned.1.call-start = ((), (), s32[]{:S(2)}) async-start(), calls=%async_computation.6 | async-start | bytes 4325376 | tf_op jit(solution)/shard_map/all_gather | solution.py:19
  11.2 11.3 %copy-start.6 = (s32[128]{0:T(128)S(1)}, s32[128]{0:T(128)}, u32[]{:S(2)}) copy-start(s32[128]{0:T(128)} %param.13) | copy-start | bytes 1540
  11.2 167.2 %all-to-all-start = ((bf16[32,128,512]{2,1,0:T(8,128)(2,1)}), bf16[32,128,512]{2,1,0:T(8,128)(2,1)}, u32[]{:S(2)}, u32[]{:S(2)}) async-start(bf16[32,128,512]{2,1,0:T(8,128)(2,1)} %stack.8), calls=%async_computation | async-start | bytes 8388608 | tf_op jit(solution)/shard_map/all_to_all | solution.py:25
  178.4 61.9 %all-to-all-start.2 = ((bf16[8,256,512]{2,1,0:T(8,128)(2,1)}), bf16[8,256,512]{2,1,0:T(8,128)(2,1)S(1)}, u32[]{:S(2)}, u32[]{:S(2)}) async-start(bf16[8,256,512]{2,1,0:T(8,128)(2,1)} %copy.89), calls=%async_computation.2 | async-start | bytes 4194304 | tf_op jit(solution)/shard_map/all_to_all | solution.py:53
  197.1 47.7 %copy-start.4 = (bf16[4,128,512]{2,1,0:T(8,128)(2,1)S(1)}, bf16[4,128,512]{2,1,0:T(8,128)(2,1)}, u32[]{:S(2)}) copy-start(bf16[4,128,512]{2,1,0:T(8,128)(2,1)} %param.11) | copy-start | bytes 1572868
  240.3 52.6 %all-to-all-start.1 = ((bf16[8,256,512]{2,1,0:T(8,128)(2,1)}), bf16[8,256,512]{2,1,0:T(8,128)(2,1)}, u32[]{:S(2)}, u32[]{:S(2)}) async-start(bf16[8,256,512]{2,1,0:T(8,128)(2,1)} %copy.86), calls=%async_computation.1 | async-start | bytes 4194304 | tf_op jit(solution)/shard_map/all_to_all | solution.py:54
  245.1 55.2 %copy-start.1 = (bf16[4,128,512]{1,2,0:T(8,128)(2,1)}, bf16[4,128,512]{1,2,0:T(8,128)(2,1)S(1)}, u32[]{:S(2)}) copy-start(bf16[4,128,512]{1,2,0:T(8,128)(2,1)S(1)} %copy.91) | copy-start | bytes 1572868
  246.6 57.0 %copy-start.5 = (bf16[4,128,512]{1,2,0:T(8,128)(2,1)}, bf16[4,128,512]{1,2,0:T(8,128)(2,1)S(1)}, u32[]{:S(2)}) copy-start(bf16[4,128,512]{1,2,0:T(8,128)(2,1)S(1)} %copy.93) | copy-start | bytes 1572868
  300.3 3.4 copy-start.3
  303.6 3.5 copy-start
  307.1 1.1 copy-start.2
  316.9 56.9 %all-to-all-start.3 = ((bf16[8,256,512]{2,1,0:T(8,128)(2,1)}), bf16[8,256,512]{2,1,0:T(8,128)(2,1)}, u32[]{:S(2)}, u32[]{:S(2)}) async-start(bf16[8,256,512]{2,1,0:T(8,128)(2,1)} %copy.97), calls=%async_computation.3 | async-start | bytes 4194304 | tf_op jit(solution)/shard_map/all_to_all | solution.py:94
  373.7 52.5 %all-to-all-start.4 = ((bf16[8,256,512]{2,1,0:T(8,128)(2,1)}), bf16[8,256,512]{2,1,0:T(8,128)(2,1)}, u32[]{:S(2)}, u32[]{:S(2)}) async-start(bf16[8,256,512]{2,1,0:T(8,128)(2,1)} %copy.102), calls=%async_computation.4 | async-start | bytes 4194304 | tf_op jit(solution)/shard_map/all_to_all | solution.py:95
  378.1 215.7 %reduce-scatter.4.cloned.1.call-start = ((), (), s32[]{:S(2)}) async-start(), calls=%async_computation.7 | async-start | bytes 8650752
Sparse Core Ops, SparseCore 0:
  9.8 158.0 all-gather.1
  457.3 136.4 reduce-scatter.3
